TPU v7x, 512 devices: a whole 4x8x8 slice. The times are simulated.
512 devices in a mesh: tok: 64 (over z, y), tp: 8 (over x, core).
Axes of the slice: x: 4, y: 8, z: 8, core: 2. Of those that a mesh axis runs over, the one named last changes fastest.
Arguments:
- activations: bfloat16 [8192, 4096], P('tok', 'tp'), may hold values from -6 to 6
- out_grad: bfloat16 [8192, 4096], P('tok', 'tp'), may hold values from -6 to 6
- routes: int32 [8192, 2], P('tok'), may hold values from 0 to 63, all different within a row; in each aligned block of 128 rows (0 to 127, 128 to 255, ...) at most 8 rows name the same one
- gate_vals: float32 [8192, 2], P('tok'), may hold values from 0.2 to 1
- w_gate: bfloat16 [64, 1536, 4096], P('tok', 'tp'), may hold values from -0.09375 to 0.09375
- w_up: bfloat16 [64, 1536, 4096], P('tok', 'tp'), may hold values from -0.09375 to 0.09375
- w_down: bfloat16 [64, 1536, 4096], P('tok', 'tp'), may hold values from -0.15625 to 0.15625
Outputs:
- in_grad: bfloat16 [8192, 4096], P('tok', 'tp')
Inputs may be any that keep to these rules, and one draw needn't show every extreme that they name: `routes`: each row names 2 different experts. In each aligned block of 128 rows (the tokens of one index of tok) no expert is named by more than 8 rows, a bound that some block reaches.
All inputs are finite; a program needn't handle non-finite values.
Results may differ from a plain program's by a relative error of at most 0.0057.
Values may be sent and summed in bfloat16 or wider, within the bound.
No kernel may reach another device: no remote copies, remote signals or barrier semaphores. Data moves between devices by JAX's collectives and lax.ppermute only.
A program may use at most 64 MiB of HBM per device.

v0:
```python
import jax
import jax.numpy as jnp
from jax import lax
from jax.sharding import PartitionSpec as P


def routing(routes, n_tok, capacity):
    tok_dev = routes.shape[0]
    top_k = routes.shape[1]
    flat = routes.reshape(-1)
    onehot = (flat[:, None] == jnp.arange(n_tok, dtype=jnp.int32)[None, :]).astype(jnp.int32)
    before = jnp.cumsum(onehot, axis=0) - onehot
    slot = jnp.sum(before * onehot, axis=1)
    position = flat * capacity + slot
    slot_count = n_tok * capacity
    hits = (position[:, None] == jnp.arange(slot_count, dtype=jnp.int32)[None, :]).astype(jnp.int32)
    hits = jnp.sum(hits.reshape(tok_dev, top_k, slot_count), axis=1)
    token_of = jnp.sum(hits * jnp.arange(tok_dev, dtype=jnp.int32)[:, None], axis=0)
    filled = jnp.sum(hits, axis=0) > 0
    return (position, token_of, filled)


def bucket(rows, token_of, filled):
    return jnp.where(filled[:, None], jnp.take(rows, token_of, axis=0), jnp.zeros((), rows.dtype))


def combine(returned, position, gate_vals):
    picked = jnp.take(returned, position, axis=0).reshape(
        gate_vals.shape[0], gate_vals.shape[1], returned.shape[1]
    )
    total = jnp.zeros((picked.shape[0], picked.shape[2]), jnp.float32)
    for column in range(gate_vals.shape[1]):
        total = total + gate_vals[:, column : column + 1] * picked[:, column].astype(jnp.float32)
    return total


def hidden_grads(gate_pre, up_pre, hidden_grad):
    sigma = jax.nn.sigmoid(gate_pre)
    silu_value = gate_pre * sigma
    slope = sigma * (1.0 + gate_pre * (1.0 - sigma))
    return (
        (hidden_grad * up_pre * slope).astype(jnp.bfloat16),
        (hidden_grad * silu_value).astype(jnp.bfloat16),
    )


def shards(activations, out_grad, routes, gate_vals, w_gate, w_up, w_down):
    n_tok = lax.axis_size("tok")
    tok_dev = routes.shape[0]
    top_k = routes.shape[1]
    capacity = max(2, 2 * tok_dev * top_k // n_tok)
    slot_count = n_tok * capacity
    gate_local = w_gate[0]
    up_local = w_up[0]
    down_local = w_down[0]
    contract_last = (((1,), (1,)), ((), ()))
    position, token_of, filled = routing(routes, n_tok, capacity)
    whole_x, whole_g = (
        lax.all_gather(activations, "tp", axis=1, tiled=True),
        lax.all_gather(out_grad, "tp", axis=1, tiled=True),
    )
    width = whole_x.shape[1]
    send_x = bucket(whole_x, token_of, filled).reshape(n_tok, capacity, width)
    send_g = bucket(whole_g, token_of, filled).reshape(n_tok, capacity, width)
    recv_x, recv_g = (
        lax.all_to_all(send_x, "tok", split_axis=0, concat_axis=0, tiled=True),
        lax.all_to_all(send_g, "tok", split_axis=0, concat_axis=0, tiled=True),
    )
    recv_x = recv_x.reshape(slot_count, width)
    recv_g = recv_g.reshape(slot_count, width)
    gate_pre = lax.dot_general(
        recv_x, gate_local, contract_last, preferred_element_type=jnp.float32
    )
    up_pre = lax.dot_general(recv_x, up_local, contract_last, preferred_element_type=jnp.float32)
    hidden_grad = lax.dot_general(
        recv_g, down_local, contract_last, preferred_element_type=jnp.float32
    )
    gate_grad, up_grad = hidden_grads(gate_pre, up_pre, hidden_grad)
    partial_value = jnp.dot(gate_grad, gate_local, preferred_element_type=jnp.float32)
    partial_value = partial_value + jnp.dot(up_grad, up_local, preferred_element_type=jnp.float32)
    partial_bf = partial_value.astype(jnp.bfloat16)
    full_width = partial_bf.shape[1]
    returned = lax.all_to_all(
        partial_bf.reshape(n_tok, capacity, full_width),
        "tok",
        split_axis=0,
        concat_axis=0,
        tiled=True,
    )
    combined = combine(returned.reshape(slot_count, full_width), position, gate_vals)
    summed = lax.psum_scatter(combined, "tp", scatter_dimension=1, tiled=True)
    return summed.astype(jnp.bfloat16)


def solution(mesh):
    placed = (
        P("tok", "tp"),
        P("tok", "tp"),
        P("tok", None),
        P("tok", None),
        P("tok", "tp", None),
        P("tok", "tp", None),
        P("tok", "tp", None),
    )
    return jax.shard_map(
        shards, mesh=mesh, in_specs=placed, out_specs=P("tok", "tp"), check_vma=False
    )
```

profile of v0, /device:TPU:16, one launch (start us, length us, event | category | flops | bytes accessed | tf_op | source)
XLA Modules:
  0.0 566.2 jit_solution(14401200045992333486)
XLA Ops:
  6.5 0.7 all-gather.3.cloned.1.call-update
  7.3 0.7 all-gather.5.cloned.1.call-update
  8.0 0.8 copy.23
  10.3 0.7 compare_and_fusion.1
  11.2 31.5 %all-gather.3.cloned.1.call-done = bf16[128,4096]{1,0:T(8,128)(2,1)} async-done(((bf16[128,512]{1,0:T(8,128)(2,1)}), bf16[128,4096]{1,0:T(8,128)(2,1)}) %all-gather.3.cloned.1.call-update) | async-done | bytes 1048592 | tf_op jit(solution)/shard_map/all_gather | solution.py:60
  42.7 9.9 %gather_fusion.1 = bf16[512,4096]{1,0:T(8,128)(2,1)} fusion(bf16[128,4096]{1,0:T(8,128)(2,1)} %all-gather.3.cloned.1.call-done, s32[1024]{0:T(1024)S(1)} %pad_clamp_fusion.1), kind=kCustom, calls=%fused_computation.clone | custom fusion | bytes 8390656 | tf_op jit(solution)/shard_map/jit(_take)/gather | solution.py:24
  52.6 20.9 %all-gather.5.cloned.1.call-done = bf16[128,4096]{1,0:T(8,128)(2,1)} async-done(((bf16[128,512]{1,0:T(8,128)(2,1)}), bf16[128,4096]{1,0:T(8,128)(2,1)}) %all-gather.5.cloned.1.call-update) | async-done | bytes 1048592 | tf_op jit(solution)/shard_map/all_gather | solution.py:59
  73.5 9.9 %gather_fusion.2 = bf16[512,4096]{1,0:T(8,128)(2,1)} fusion(bf16[128,4096]{1,0:T(8,128)(2,1)} %all-gather.5.cloned.1.call-done, s32[1024]{0:T(1024)S(1)} %pad_clamp_fusion.1), kind=kCustom, calls=%fused_computation.1.clone | custom fusion | bytes 8390656 | tf_op jit(solution)/shard_map/jit(_take)/gather | solution.py:24
  83.4 5.4 fusion.7
  88.8 109.8 %all_to_all.15 = bf16[64,8,4096]{2,1,0:T(8,128)(2,1)} all-to-all(bf16[64,8,4096]{2,1,0:T(8,128)(2,1)S(1)} %get-tuple-element.12), channel_id=1, replica_groups=mesh['tok'=64,'tp'=8] {'tok'}, dimensions={0} | all-to-all | bytes 8388608 | tf_op jit(solution)/shard_map/all_to_all | solution.py:66
  198.5 16.3 %all-to-all-start = ((bf16[64,8,4096]{2,1,0:T(8,128)(2,1)}), bf16[64,8,4096]{2,1,0:T(8,128)(2,1)}, u32[]{:S(2)}, u32[]{:S(2)}) async-start(bf16[64,8,4096]{2,1,0:T(8,128)(2,1)} %get-tuple-element.13), calls=%async_computation | async-start | bytes 8388608 | tf_op jit(solution)/shard_map/all_to_all | solution.py:67
  214.9 3.7 fusion.1
  218.6 114.2 %all-to-all-done = bf16[64,8,4096]{2,1,0:T(8,128)(2,1)} async-done(((bf16[64,8,4096]{2,1,0:T(8,128)(2,1)}), bf16[64,8,4096]{2,1,0:T(8,128)(2,1)}, u32[]{:S(2)}, u32[]{:S(2)}) %all-to-all-start) | async-done | bytes 4194336 | tf_op jit(solution)/shard_map/all_to_all | solution.py:67
  332.8 5.0 fusion.5
  337.8 8.3 %fusion.10 = f32[512,4096]{1,0:T(8,128)} fusion(bf16[1,192,4096]{2,1,0:T(8,128)(2,1)S(1)} %copy-done.1, f32[512,192]{0,1:T(8,128)} %fusion.5, bf16[1,192,4096]{2,1,0:T(8,128)(2,1)S(1)} %copy-done, bf16[64,8,4096]{2,1,0:T(8,128)(2,1)} %all_to_all.15, f32[512,192]{0,1:T(8,128)S(1)} %fusion.1), kind=kOutput, calls=%fused_computation.19 | convolution fusion | flops 1611595776 | bytes 16515072 | tf_op jit(solution)/shard_map/dot_general | solution.py:79
  346.1 6.8 %fusion = bf16[64,8,4096]{2,1,0:T(8,128)(2,1)} fusion(f32[512,4096]{1,0:T(8,128)} %fusion.10, bf16[1,192,4096]{2,1,0:T(8,128)(2,1)S(1)} %copy-done, f32[512,192]{0,1:T(8,128)} %fusion.5, f32[512,192]{0,1:T(8,128)S(1)} %fusion.1), kind=kOutput, calls=%fused_computation.4 | convolution fusion | flops 810090496 | bytes 14942208 | tf_op jit(solution)/shard_map/dot_general | solution.py:80
  353.0 15.8 %all-to-all-start.2 = ((bf16[64,8,4096]{2,1,0:T(8,128)(2,1)}), bf16[64,8,4096]{2,1,0:T(8,128)(2,1)}, u32[]{:S(2)}, u32[]{:S(2)}) async-start(bf16[64,8,4096]{2,1,0:T(8,128)(2,1)} %fusion), calls=%async_computation.2 | async-start | bytes 8388608 | tf_op jit(solution)/shard_map/all_to_all | solution.py:83
  369.4 110.9 %all-to-all-done.2 = bf16[64,8,4096]{2,1,0:T(8,128)(2,1)} async-done(((bf16[64,8,4096]{2,1,0:T(8,128)(2,1)}), bf16[64,8,4096]{2,1,0:T(8,128)(2,1)}, u32[]{:S(2)}, u32[]{:S(2)}) %all-to-all-start.2) | async-done | bytes 4194336 | tf_op jit(solution)/shard_map/all_to_all | solution.py:83
  480.3 7.9 %gather_fusion = bf16[256,4096]{1,0:T(8,128)(2,1)} fusion(bf16[512,4096]{1,0:T(8,128)(2,1)} %bitcast.10, s32[1024]{0:T(1024)S(1)} %pad_clamp_fusion), kind=kCustom, calls=%fused_computation.2 | custom fusion | bytes 4195328 | tf_op jit(solution)/shard_map/jit(_take)/gather | solution.py:28
  488.3 4.4 gather.10
  492.7 4.0 copy_select_fusion
  496.7 1.8 fusion.9
  498.5 59.6 %reduce-scatter.2.cloned.1.call-done = f32[128,512]{1,0:T(8,128)} async-done(((f32[128,4096]{1,0:T(8,128)}), f32[128,512]{1,0:T(8,128)}) %reduce-scatter.2.cloned.1.call-update) | async-done | bytes 262160 | tf_op jit(solution)/shard_map/reduce_scatter | solution.py:91
  558.1 1.6 convert_element_type.45
  (33 shorter events, 2.2 us)
Async XLA Ops:
  6.5 331.3 %copy-start = (bf16[1,192,4096]{2,1,0:T(8,128)(2,1)S(1)}, bf16[1,192,4096]{2,1,0:T(8,128)(2,1)}, u32[]{:S(2)}) copy-start(bf16[1,192,4096]{2,1,0:T(8,128)(2,1)} %param.14) | copy-start | bytes 4718596
  6.5 36.1 %all-gather.3.cloned.1.call-start = ((), (), s32[]{:S(2)}) async-start(), calls=%async_computation.4 | async-start | bytes 1179648 | tf_op jit(solution)/shard_map/all_gather | solution.py:60
  7.3 66.2 %all-gather.5.cloned.1.call-start = ((), (), s32[]{:S(2)}) async-start(), calls=%async_computation.5 | async-start | bytes 1179648 | tf_op jit(solution)/shard_map/all_gather | solution.py:59
  198.5 16.4 %copy-start.1 = (bf16[1,192,4096]{2,1,0:T(8,128)(2,1)S(1)}, bf16[1,192,4096]{2,1,0:T(8,128)(2,1)}, u32[]{:S(2)}) copy-start(bf16[1,192,4096]{2,1,0:T(8,128)(2,1)} %param.13) | copy-start | bytes 4718596
  198.5 134.3 %all-to-all-start = ((bf16[64,8,4096]{2,1,0:T(8,128)(2,1)}), bf16[64,8,4096]{2,1,0:T(8,128)(2,1)}, u32[]{:S(2)}, u32[]{:S(2)}) async-start(bf16[64,8,4096]{2,1,0:T(8,128)(2,1)} %get-tuple-element.13), calls=%async_computation | async-start | bytes 8388608 | tf_op jit(solution)/shard_map/all_to_all | solution.py:67
  353.0 16.1 %copy-start.2 = (s32[128,2]{0,1:T(2,128)S(1)}, s32[128,2]{0,1:T(2,128)}, u32[]{:S(2)}) copy-start(s32[128,2]{0,1:T(2,128)} %param.11) | copy-start | bytes 3076
  353.0 16.4 %copy-start.3 = (f32[128,2]{0,1:T(2,128)S(1)}, f32[128,2]{0,1:T(2,128)}, u32[]{:S(2)}) copy-start(f32[128,2]{0,1:T(2,128)} %param.12) | copy-start | bytes 3076
  353.0 127.4 %all-to-all-start.2 = ((bf16[64,8,4096]{2,1,0:T(8,128)(2,1)}), bf16[64,8,4096]{2,1,0:T(8,128)(2,1)}, u32[]{:S(2)}, u32[]{:S(2)}) async-start(bf16[64,8,4096]{2,1,0:T(8,128)(2,1)} %fusion), calls=%async_computation.2 | async-start | bytes 8388608 | tf_op jit(solution)/shard_map/all_to_all | solution.py:83
  368.8 189.3 %reduce-scatter.2.cloned.1.call-start = ((), (), s32[]{:S(2)}) async-start(), calls=%async_computation.6 | async-start | bytes 2359296 | tf_op jit(solution)/shard_map/reduce_scatter | solution.py:91
Sparse Core Ops, SparseCore 0:
  9.5 33.1 all-gather.2
  44.8 28.5 all-gather.4
  498.6 59.3 reduce-scatter.1
where the time goes:
time: 567 us; the launch traced here: 566 us
  waiting for transfers between devices  338 us (60%)
  blocking collectives  110 us (19%)
  local copies, waits for them, and re-layouts  33.9 us (6%)
  starting transfers between devices  32.5 us (6%)
  matrix products  23.8 us (4%)
  other arithmetic  14.5 us (3%)
  between operations  13.2 us (2%)
    all_to_all x1, waiting for transfers between devices, shards(): lax.all_to_all(send_g, 'tok', split_axis=0, concat_axis=0, tiled=True)  114 us
    all_to_all x1, waiting for transfers between devices, shards(): lax.all_to_all(partial_bf.reshape(n_tok, capacity, full_width), 'tok', sp...  111 us
    all_to_all x1, blocking collectives, shards(): lax.all_to_all(send_x, 'tok', split_axis=0, concat_axis=0, tiled=True)  110 us
    reduce_scatter x1, waiting for transfers between devices, shards(): summed = lax.psum_scatter(combined, 'tp', scatter_dimension=1, tiled=True)  59.6 us
    all_gather x1, waiting for transfers between devices, shards(): lax.all_gather(out_grad, 'tp', axis=1, tiled=True)  31.5 us
    all_gather x1, waiting for transfers between devices, shards(): lax.all_gather(activations, 'tp', axis=1, tiled=True)  20.9 us
    gather x2, local copies, waits for them, and re-layouts, bucket(): jnp.take(rows, token_of, axis=0)  19.8 us
    all_to_all x1, starting transfers between devices, shards(): lax.all_to_all(send_g, 'tok', split_axis=0, concat_axis=0, tiled=True)  16.3 us
  transfers between devices with their start and end apart: 5, of which 5 were waited for; matrix products, arithmetic and copies ran while one was open for 3% of the time, Pallas kernels for 0%

commit v1 on v0

--- a/solution.py
+++ b/solution.py
@@ -2,6 +2,27 @@
 import jax.numpy as jnp
 from jax import lax
 from jax.sharding import PartitionSpec as P
+
+
+def ring_gather(shard, axis, dim):
+    peers, position, rows = (lax.axis_size(axis), lax.axis_index(axis), shard.shape[dim])
+    right = [(i, (i + 1) % peers) for i in range(peers)]
+    left = [(i, (i - 1) % peers) for i in range(peers)]
+    filled = jnp.zeros((*shard.shape[:dim], peers * rows, *shard.shape[dim + 1 :]), shard.dtype)
+    filled = lax.dynamic_update_slice_in_dim(filled, shard, position * rows, axis=dim)
+    from_left = from_right = shard
+    half = peers // 2
+    for hop in range(1, half + 1):
+        from_left = lax.ppermute(from_left, axis, right)
+        filled = lax.dynamic_update_slice_in_dim(
+            filled, from_left, (position - hop) % peers * rows, axis=dim
+        )
+        if hop < peers - half:
+            from_right = lax.ppermute(from_right, axis, left)
+            filled = lax.dynamic_update_slice_in_dim(
+                filled, from_right, (position + hop) % peers * rows, axis=dim
+            )
+    return filled
 
 
 def routing(routes, n_tok, capacity):
@@ -56,7 +77,7 @@
     contract_last = (((1,), (1,)), ((), ()))
     position, token_of, filled = routing(routes, n_tok, capacity)
     whole_x, whole_g = (
-        lax.all_gather(activations, "tp", axis=1, tiled=True),
+        ring_gather(activations, "tp", 1),
         lax.all_gather(out_grad, "tp", axis=1, tiled=True),
     )
     width = whole_x.shape[1]

time: 567 us -> 539 us (0.951)
  the two profiles are of different devices: /device:TPU:16 before, /device:TPU:8 now
where the time goes in v1:
time: 539 us; the launch traced here: 538 us
  waiting for transfers between devices  304 us (56%)
  blocking collectives  111 us (21%)
  starting transfers between devices  42.2 us (8%)
  local copies, waits for them, and re-layouts  28.6 us (5%)
  matrix products  23.8 us (4%)
  other arithmetic  14.5 us (3%)
  between operations  13.8 us (3%)
    all_to_all x1, waiting for transfers between devices, shards(): lax.all_to_all(send_g, 'tok', split_axis=0, concat_axis=0, tiled=True)  114 us
    all_to_all x1, waiting for transfers between devices, shards(): lax.all_to_all(partial_bf.reshape(n_tok, capacity, full_width), 'tok', sp...  112 us
    all_to_all x1, blocking collectives, shards(): lax.all_to_all(send_x, 'tok', split_axis=0, concat_axis=0, tiled=True)  111 us
    reduce_scatter x1, waiting for transfers between devices, shards(): summed = lax.psum_scatter(combined, 'tp', scatter_dimension=1, tiled=True)  58.9 us
    all_to_all x1, starting transfers between devices, shards(): lax.all_to_all(partial_bf.reshape(n_tok, capacity, full_width), 'tok', sp...  17.8 us
    all_to_all x1, starting transfers between devices, shards(): lax.all_to_all(send_g, 'tok', split_axis=0, concat_axis=0, tiled=True)  15.3 us
    gather x2, local copies, waits for them, and re-layouts, bucket(): jnp.take(rows, token_of, axis=0)  14.3 us
    gather x2, local copies, waits for them, and re-layouts, combine(): jnp.take(returned, position, axis=0)  12.3 us
  transfers between devices with their start and end apart: 11, of which 7 were waited for; matrix products, arithmetic and copies ran while one was open for 2% of the time, Pallas kernels for 0%

profile of v1, /device:TPU:8, one launch (start us, length us, event | category | flops | bytes accessed | tf_op | source)
XLA Modules:
  0.0 538.1 jit_solution(11801640819723863419)
XLA Ops:
  6.6 2.9 collective-permute-start.1
  13.0 2.9 collective-permute-start.3
  16.0 2.6 collective-permute-done.2
  18.6 3.0 collective-permute-start.5
  21.6 2.6 collective-permute-done.4
  24.3 5.5 %collective-permute-done.6 = bf16[128,512]{1,0:T(8,128)(2,1)S(1)} collective-permute-done((bf16[128,512]{1,0:T(8,128)(2,1)S(1)}, bf16[128,512]{1,0:T(8,128)(2,1)S(1)}, u32[]{:S(2)}, u32[]{:S(2)}) %collective-permute-start.6) | collective-permute-done | bytes 131104 | tf_op jit(solution)/shard_map/ppermute | solution.py:16
  29.8 4.4 gather_fusion.2
  34.2 8.5 %all-gather.2.cloned.1.call-done = bf16[128,4096]{1,0:T(8,128)(2,1)} async-done(((bf16[128,512]{1,0:T(8,128)(2,1)}), bf16[128,4096]{1,0:T(8,128)(2,1)}) %all-gather.2.cloned.1.call-update) | async-done | bytes 1048592 | tf_op jit(solution)/shard_map/all_gather | solution.py:81
  42.8 9.9 %gather_fusion.1 = bf16[512,4096]{1,0:T(8,128)(2,1)} fusion(bf16[128,4096]{1,0:T(8,128)(2,1)} %all-gather.2.cloned.1.call-done, s32[1024]{0:T(1024)S(1)} %pad_clamp_fusion.1), kind=kCustom, calls=%fused_computation.clone | custom fusion | bytes 8390656 | tf_op jit(solution)/shard_map/jit(_take)/gather | solution.py:45
  52.7 5.3 fusion.7
  58.1 111.0 %all_to_all.15 = bf16[64,8,4096]{2,1,0:T(8,128)(2,1)} all-to-all(bf16[64,8,4096]{2,1,0:T(8,128)(2,1)S(1)} %get-tuple-element.12), channel_id=1, replica_groups=mesh['tok'=64,'tp'=8] {'tok'}, dimensions={0} | all-to-all | bytes 8388608 | tf_op jit(solution)/shard_map/all_to_all | solution.py:87
  169.1 15.3 %all-to-all-start = ((bf16[64,8,4096]{2,1,0:T(8,128)(2,1)}), bf16[64,8,4096]{2,1,0:T(8,128)(2,1)}, u32[]{:S(2)}, u32[]{:S(2)}) async-start(bf16[64,8,4096]{2,1,0:T(8,128)(2,1)} %get-tuple-element.13), calls=%async_computation | async-start | bytes 8388608 | tf_op jit(solution)/shard_map/all_to_all | solution.py:88
  184.4 3.7 fusion.1
  188.1 114.1 %all-to-all-done = bf16[64,8,4096]{2,1,0:T(8,128)(2,1)} async-done(((bf16[64,8,4096]{2,1,0:T(8,128)(2,1)}), bf16[64,8,4096]{2,1,0:T(8,128)(2,1)}, u32[]{:S(2)}, u32[]{:S(2)}) %all-to-all-start) | async-done | bytes 4194336 | tf_op jit(solution)/shard_map/all_to_all | solution.py:88
  302.2 5.0 fusion.5
  307.2 8.3 %fusion.10 = f32[512,4096]{1,0:T(8,128)} fusion(bf16[1,192,4096]{2,1,0:T(8,128)(2,1)S(1)} %copy-done.1, f32[512,192]{0,1:T(8,128)} %fusion.5, bf16[1,192,4096]{2,1,0:T(8,128)(2,1)S(1)} %copy-done, bf16[64,8,4096]{2,1,0:T(8,128)(2,1)} %all_to_all.15, f32[512,192]{0,1:T(8,128)S(1)} %fusion.1), kind=kOutput, calls=%fused_computation.19 | convolution fusion | flops 1611595776 | bytes 16515072 | tf_op jit(solution)/shard_map/dot_general | solution.py:100
  315.5 6.8 %fusion = bf16[64,8,4096]{2,1,0:T(8,128)(2,1)} fusion(f32[512,4096]{1,0:T(8,128)} %fusion.10, bf16[1,192,4096]{2,1,0:T(8,128)(2,1)S(1)} %copy-done, f32[512,192]{0,1:T(8,128)} %fusion.5, f32[512,192]{0,1:T(8,128)S(1)} %fusion.1), kind=kOutput, calls=%fused_computation.4 | convolution fusion | flops 810090496 | bytes 14942208 | tf_op jit(solution)/shard_map/dot_general | solution.py:101
  322.3 17.8 %all-to-all-start.2 = ((bf16[64,8,4096]{2,1,0:T(8,128)(2,1)}), bf16[64,8,4096]{2,1,0:T(8,128)(2,1)}, u32[]{:S(2)}, u32[]{:S(2)}) async-start(bf16[64,8,4096]{2,1,0:T(8,128)(2,1)} %fusion), calls=%async_computation.2 | async-start | bytes 8388608 | tf_op jit(solution)/shard_map/all_to_all | solution.py:104
  340.7 111.9 %all-to-all-done.2 = bf16[64,8,4096]{2,1,0:T(8,128)(2,1)} async-done(((bf16[64,8,4096]{2,1,0:T(8,128)(2,1)}), bf16[64,8,4096]{2,1,0:T(8,128)(2,1)}, u32[]{:S(2)}, u32[]{:S(2)}) %all-to-all-start.2) | async-done | bytes 4194336 | tf_op jit(solution)/shard_map/all_to_all | solution.py:104
  452.6 7.9 %gather_fusion = bf16[256,4096]{1,0:T(8,128)(2,1)} fusion(bf16[512,4096]{1,0:T(8,128)(2,1)} %bitcast.10, s32[1024]{0:T(1024)S(1)} %pad_clamp_fusion), kind=kCustom, calls=%fused_computation.2 | custom fusion | bytes 4195328 | tf_op jit(solution)/shard_map/jit(_take)/gather | solution.py:49
  460.5 4.4 gather.10
  464.9 4.0 copy_select_fusion
  468.9 1.8 fusion.9
  470.7 58.9 %reduce-scatter.2.cloned.1.call-done = f32[128,512]{1,0:T(8,128)} async-done(((f32[128,4096]{1,0:T(8,128)}), f32[128,512]{1,0:T(8,128)}) %reduce-scatter.2.cloned.1.call-update) | async-done | bytes 262160 | tf_op jit(solution)/shard_map/reduce_scatter | solution.py:112
  (55 shorter events, 5.6 us)
Async XLA Ops:
  6.5 300.7 %copy-start = (bf16[1,192,4096]{2,1,0:T(8,128)(2,1)S(1)}, bf16[1,192,4096]{2,1,0:T(8,128)(2,1)}, u32[]{:S(2)}) copy-start(bf16[1,192,4096]{2,1,0:T(8,128)(2,1)} %param.14) | copy-start | bytes 4718596
  6.5 6.4 %copy-start.2 = (bf16[128,512]{1,0:T(8,128)(2,1)S(1)}, bf16[128,512]{1,0:T(8,128)(2,1)}, u32[]{:S(2)}) copy-start(bf16[128,512]{1,0:T(8,128)(2,1)} %param.9) | copy-start | bytes 393220
  6.5 36.2 %all-gather.2.cloned.1.call-start = ((), (), s32[]{:S(2)}) async-start(), calls=%async_computation.4 | async-start | bytes 1179648 | tf_op jit(solution)/shard_map/all_gather | solution.py:81
  6.5 6.4 %collective-permute-start = (bf16[128,512]{1,0:T(8,128)(2,1)}, bf16[128,512]{1,0:T(8,128)(2,1)S(1)}, u32[]{:S(2)}, u32[]{:S(2)}) collective-permute-start(bf16[128,512]{1,0:T(8,128)(2,1)} %param.9), channel_id=1, source_target_pairs={{0,1},{1,2},{2,3},{3,4},{4,5},{5,6},{6,7},{7,0},{8,9},{9,10},{10,1... | collective-permute-start | bytes 393224 | tf_op jit(solution)/shard_map/ppermute | solution.py:16
  6.6 6.5 %collective-permute-start.1 = (bf16[128,512]{1,0:T(8,128)(2,1)}, bf16[128,512]{1,0:T(8,128)(2,1)S(1)}, u32[]{:S(2)}, u32[]{:S(2)}) collective-permute-start(bf16[128,512]{1,0:T(8,128)(2,1)} %param.9), channel_id=1, source_target_pairs={{0,7},{1,0},{2,1},{3,2},{4,3},{5,4},{6,5},{7,6},{8,15},{9,8},{10,9... | collective-permute-start | bytes 393224 | tf_op jit(solution)/shard_map/ppermute | solution.py:21
  13.0 5.6 %collective-permute-start.2 = (bf16[128,512]{1,0:T(8,128)(2,1)S(1)}, bf16[128,512]{1,0:T(8,128)(2,1)S(1)}, u32[]{:S(2)}, u32[]{:S(2)}) collective-permute-start(bf16[128,512]{1,0:T(8,128)(2,1)S(1)} %collective-permute-done), channel_id=1, source_target_pairs={{0,1},{1,2},{2,3},{3,4},{4,5},{5,6},{6,7},{7,0},{8,9},{9,10},{10,1... | collective-permute-start | bytes 393224 | tf_op jit(solution)/shard_map/ppermute | solution.py:16
  13.0 5.6 %collective-permute-start.3 = (bf16[128,512]{1,0:T(8,128)(2,1)S(1)}, bf16[128,512]{1,0:T(8,128)(2,1)S(1)}, u32[]{:S(2)}, u32[]{:S(2)}) collective-permute-start(bf16[128,512]{1,0:T(8,128)(2,1)S(1)} %collective-permute-done.1), channel_id=1, source_target_pairs={{0,7},{1,0},{2,1},{3,2},{4,3},{5,4},{6,5},{7,6},{8,15},{9,8},{10,9... | collective-permute-start | bytes 393224 | tf_op jit(solution)/shard_map/ppermute | solution.py:21
  18.6 5.6 %collective-permute-start.4 = (bf16[128,512]{1,0:T(8,128)(2,1)S(1)}, bf16[128,512]{1,0:T(8,128)(2,1)S(1)}, u32[]{:S(2)}, u32[]{:S(2)}) collective-permute-start(bf16[128,512]{1,0:T(8,128)(2,1)S(1)} %collective-permute-done.2), channel_id=1, source_target_pairs={{0,1},{1,2},{2,3},{3,4},{4,5},{5,6},{6,7},{7,0},{8,9},{9,10},{10,1... | collective-permute-start | bytes 393224 | tf_op jit(solution)/shard_map/ppermute | solution.py:16
  18.6 5.6 %collective-permute-start.5 = (bf16[128,512]{1,0:T(8,128)(2,1)S(1)}, bf16[128,512]{1,0:T(8,128)(2,1)S(1)}, u32[]{:S(2)}, u32[]{:S(2)}) collective-permute-start(bf16[128,512]{1,0:T(8,128)(2,1)S(1)} %collective-permute-done.3), channel_id=1, source_target_pairs={{0,7},{1,0},{2,1},{3,2},{4,3},{5,4},{6,5},{7,6},{8,15},{9,8},{10,9... | collective-permute-start | bytes 393224 | tf_op jit(solution)/shard_map/ppermute | solution.py:21
  24.2 5.6 %collective-permute-start.6 = (bf16[128,512]{1,0:T(8,128)(2,1)S(1)}, bf16[128,512]{1,0:T(8,128)(2,1)S(1)}, u32[]{:S(2)}, u32[]{:S(2)}) collective-permute-start(bf16[128,512]{1,0:T(8,128)(2,1)S(1)} %collective-permute-done.4), channel_id=1, source_target_pairs={{0,1},{1,2},{2,3},{3,4},{4,5},{5,6},{6,7},{7,0},{8,9},{9,10},{10,1... | collective-permute-start | bytes 393224 | tf_op jit(solution)/shard_map/ppermute | solution.py:16
  169.1 15.3 %copy-start.1 = (bf16[1,192,4096]{2,1,0:T(8,128)(2,1)S(1)}, bf16[1,192,4096]{2,1,0:T(8,128)(2,1)}, u32[]{:S(2)}) copy-start(bf16[1,192,4096]{2,1,0:T(8,128)(2,1)} %param.13) | copy-start | bytes 4718596
  169.1 133.2 %all-to-all-start = ((bf16[64,8,4096]{2,1,0:T(8,128)(2,1)}), bf16[64,8,4096]{2,1,0:T(8,128)(2,1)}, u32[]{:S(2)}, u32[]{:S(2)}) async-start(bf16[64,8,4096]{2,1,0:T(8,128)(2,1)} %get-tuple-element.13), calls=%async_computation | async-start | bytes 8388608 | tf_op jit(solution)/shard_map/all_to_all | solution.py:88
  322.3 18.0 %copy-start.3 = (s32[128,2]{0,1:T(2,128)S(1)}, s32[128,2]{0,1:T(2,128)}, u32[]{:S(2)}) copy-start(s32[128,2]{0,1:T(2,128)} %param.11) | copy-start | bytes 3076
  322.3 18.3 %copy-start.4 = (f32[128,2]{0,1:T(2,128)S(1)}, f32[128,2]{0,1:T(2,128)}, u32[]{:S(2)}) copy-start(f32[128,2]{0,1:T(2,128)} %param.12) | copy-start | bytes 3076
  322.3 130.3 %all-to-all-start.2 = ((bf16[64,8,4096]{2,1,0:T(8,128)(2,1)}), bf16[64,8,4096]{2,1,0:T(8,128)(2,1)}, u32[]{:S(2)}, u32[]{:S(2)}) async-start(bf16[64,8,4096]{2,1,0:T(8,128)(2,1)} %fusion), calls=%async_computation.2 | async-start | bytes 8388608 | tf_op jit(solution)/shard_map/all_to_all | solution.py:104
  340.1 189.6 %reduce-scatter.2.cloned.1.call-start = ((), (), s32[]{:S(2)}) async-start(), calls=%async_computation.5 | async-start | bytes 2359296 | tf_op jit(solution)/shard_map/reduce_scatter | solution.py:112
Sparse Core Ops, SparseCore 0:
  9.6 33.0 all-gather.1
  470.8 58.7 reduce-scatter.1
